TPU v7x, 256 devices: a whole 4x4x8 slice. The times are simulated.
256 devices in a mesh: group: 16 (over z, core), blk: 16 (over y, x).
Axes of the slice: x: 4, y: 4, z: 8, core: 2. Of those that a mesh axis runs over, the one named last changes fastest.
Arguments:
- hamiltonian: bfloat16 [4096, 18, 64, 256], P(('group', 'blk')), may hold values from -0.09375 to 0.09375
- block_columns: int32 [4096, 18, 4], P(('group', 'blk')), may hold values from 0 to 15, as said below
- potential: float32 [262144], P(('group', 'blk')), may hold values from -1 to 1
- trial_slab: float32 [262144, 128], P(('group', 'blk')), may hold values from -40 to 40
Outputs:
- ortho_slab: float32 [262144, 128], P(('group', 'blk'))
- upper_factor: float32 [128, 128], replicated
Inputs may be any that keep to these rules, and one draw needn't show every extreme that they name: `block_columns`: for each row block and each source, the 4 entries are distinct.
All inputs are finite; a program needn't handle non-finite values.
Results may differ from a plain program's by a relative error of at most 0.0021.
Values may be sent and summed in bfloat16 or wider, within the bound.
A program may use at most 64 MiB of HBM per device.

v0:
```python
import jax
import jax.numpy as jnp
from jax import lax
from jax.sharding import PartitionSpec as P

precise = lax.Precision.HIGHEST


def neighbours(block):
    count = lax.axis_size("group")
    forward = [(i, i + 1) for i in range(count - 1)]
    backward = [(i + 1, i) for i in range(count - 1)]
    below = lax.ppermute(block, "group", forward)
    above = lax.ppermute(block, "group", backward)
    return (below, above)


def couple_all(hamiltonian, block_columns, rounded):
    shard_blocks, nsrc, block_size, width = hamiltonian.shape
    per_source = block_columns.shape[2]
    states = rounded.shape[2]
    gathered = lax.all_gather(rounded, "blk", axis=0, tiled=True)
    below, above = neighbours(rounded)
    table = jnp.concatenate([gathered, below, above], axis=0)
    offsets = (jnp.arange(nsrc, dtype=jnp.int32) * shard_blocks)[None, :, None]
    index = block_columns + offsets
    picked = table[index.reshape(-1)].reshape(shard_blocks, nsrc, per_source * block_size, states)
    return jnp.einsum("rsik,rskn->rin", hamiltonian, picked, preferred_element_type=jnp.float32)


def on_device(hamiltonian, block_columns, potential, trial_slab):
    shard_blocks = hamiltonian.shape[0]
    block_size = hamiltonian.shape[2]
    states = trial_slab.shape[1]
    start_slab = trial_slab.reshape(shard_blocks, block_size, states)
    weights = potential.reshape(shard_blocks, block_size, 1)
    coupled_start = couple_all(hamiltonian, block_columns, start_slab.astype(jnp.bfloat16))
    filtered_once = 0.5 * (coupled_start + weights * start_slab)
    coupled_next = couple_all(hamiltonian, block_columns, filtered_once.astype(jnp.bfloat16))
    filtered = coupled_next + weights * filtered_once - start_slab
    flat = filtered.reshape(shard_blocks * block_size, states)
    rows_total = flat.shape[0] * lax.axis_size("group") * lax.axis_size("blk")
    local_gram = jnp.dot(flat.T, flat, precision=precise)
    gram = lax.psum(local_gram, ("group", "blk")) / rows_total
    lower = jnp.linalg.cholesky(gram)
    ortho_slab = lax.linalg.triangular_solve(
        lower, flat, left_side=False, lower=True, transpose_a=True
    )
    return (ortho_slab, jnp.transpose(lower))


def solution(mesh):
    placed = (
        P(("group", "blk"), None, None, None),
        P(("group", "blk"), None, None),
        P(("group", "blk")),
        P(("group", "blk"), None),
    )
    return jax.shard_map(
        on_device,
        mesh=mesh,
        in_specs=placed,
        out_specs=(P(("group", "blk"), None), P()),
        check_vma=False,
    )
```

profile of v0, /device:TPU:1, one launch (start us, length us, event | category | flops | bytes accessed | tf_op | source)
XLA Modules:
  0.0 493.7 jit_solution(8105677238921476546)
XLA Ops:
  7.2 1.8 convert_element_type.6
  9.1 5.1 %collective-permute-start.1 = (bf16[16,64,128]{2,1,0:T(8,128)(2,1)}, bf16[16,64,128]{2,1,0:T(8,128)(2,1)S(1)}, u32[]{:S(2)}, u32[]{:S(2)}) collective-permute-start(bf16[16,64,128]{2,1,0:T(8,128)(2,1)} %convert_element_type.6), channel_id=1, source_target_pairs={{16,0},{32,16},{48,32},{64,48},{80,64},{96,80},{112,96},{128,112},... | collective-permute-start | bytes 786440 | tf_op jit(solution)/shard_map/ppermute | solution.py:14
  14.2 1.9 collective-permute-start
  16.2 0.8 broadcast_add_fusion
  18.3 1.5 collective-permute-done
  19.8 51.6 %all-gather.3.cloned.1.call-done = bf16[256,64,128]{2,1,0:T(8,128)(2,1)} async-done(((bf16[16,64,128]{2,1,0:T(8,128)(2,1)}), bf16[256,64,128]{2,1,0:T(8,128)(2,1)}) %all-gather.3.cloned.1.call-update) | async-done | bytes 4194320 | tf_op jit(solution)/shard_map/all_gather | solution.py:22
  71.4 4.2 pad_maximum_fusion
  75.5 29.1 %gather_fusion = bf16[1152,64,128]{2,1,0:T(8,128)(2,1)} fusion(bf16[288,64,128]{2,1,0:T(8,128)(2,1)} %pad_maximum_fusion, s32[2048]{0:T(1024)S(1)} %pad_clamp_fusion), kind=kCustom, calls=%fused_computation | custom fusion | bytes 37753344 | tf_op jit(solution)/shard_map/gather | solution.py:27
  104.6 13.5 %multiply_convert_fusion = (bf16[16,64,128]{2,1,0:T(8,128)(2,1)}, f32[16,64,128]{2,1,0:T(8,128)S(1)}) fusion(f32[16,64,128]{2,1,0:T(8,128)S(1)} %bitcast.44, f32[16,64]{1,0:T(8,128)S(1)} %mul.37, bf16[16,18,64,256]{3,2,1,0:T(8,128)(2,1)} %param.4, bf16[16,18,256,128]{3,2,1,0:T(8,128)(2,1)} %bitcast.41), kind=kOutput, calls=%fused_computation.10 | convolution fusion | flops 1208483840 | bytes 29626368 | tf_op jit(solution)/shard_map/rsik,rskn->rin/dot_general | solution.py:28
  118.2 2.6 collective-permute-start.3
  120.8 3.3 collective-permute-start.2
  124.1 2.1 collective-permute-done.3
  126.2 1.3 collective-permute-done.2
  127.5 47.1 %all-gather.5.cloned.1.call-done = bf16[256,64,128]{2,1,0:T(8,128)(2,1)} async-done(((bf16[16,64,128]{2,1,0:T(8,128)(2,1)}), bf16[256,64,128]{2,1,0:T(8,128)(2,1)}) %all-gather.5.cloned.1.call-update) | async-done | bytes 4194320 | tf_op jit(solution)/shard_map/all_gather | solution.py:22
  174.6 4.2 pad_maximum_fusion.1
  178.8 29.2 %gather_fusion.1 = bf16[1152,64,128]{2,1,0:T(8,128)(2,1)} fusion(bf16[288,64,128]{2,1,0:T(8,128)(2,1)} %pad_maximum_fusion.1, s32[2048]{0:T(1024)S(1)} %pad_clamp_fusion), kind=kCustom, calls=%fused_computation.1 | custom fusion | bytes 37753344 | tf_op jit(solution)/shard_map/gather | solution.py:27
  208.0 12.8 %fusion.2 = f32[16,64,128]{2,1,0:T(8,128)S(1)} fusion(f32[16,64,128]{2,1,0:T(8,128)S(1)} %bitcast.45, bf16[16,18,64,256]{3,2,1,0:T(8,128)(2,1)} %param.4, bf16[16,18,256,128]{3,2,1,0:T(8,128)(2,1)} %bitcast.40, f32[16,64,128]{2,1,0:T(8,128)S(1)} %get-tuple-element.11, f32[16,64]{1,0:T(8,128)S(1)} %broadcast_multiply_fusion.1), kind=kOutput, calls=%fused_computation.8 | convolution fusion | flops 1208352768 | bytes 29888512 | tf_op jit(solution)/shard_map/rsik,rskn->rin/dot_general | solution.py:28
  220.8 1.6 convolution_bitcast_fusion.2
  222.5 237.9 %all-reduce.2.cloned.1.call-done = f32[128,128]{0,1:T(8,128)} async-done(((f32[128,128]{0,1:T(8,128)}), f32[128,128]{0,1:T(8,128)}) %all-reduce.2.cloned.1.call-update) | async-done | bytes 65552 | tf_op jit(solution)/shard_map/psum | solution.py:44
  460.4 0.8 broadcast_multiply_fusion
  461.4 0.9 fusion.5
  462.2 11.7 %cholesky.16 = f32[128,128]{1,0:T(8,128)S(1)} custom-call(f32[128,128]{1,0:T(8,128)S(1)} %fusion.5), custom_call_target="Cholesky" | custom-call | tf_op jit(solution)/shard_map/jit(cholesky)/cholesky | solution.py:45
  476.0 9.8 %custom-call.6 = f32[1,128,128]{1,2,0:T(8,128)S(1)} custom-call(f32[1,128,128]{2,1,0:T(8,128)S(1)} %get-tuple-element.9), custom_call_target="InvertDiagBlocksLowerTriangular" | custom-call | tf_op jit(solution)/shard_map/triangular_solve | solution.py:46
  485.8 1.4 fusion.3
  (21 shorter events, 3.7 us)
Async XLA Ops:
  7.2 64.2 %all-gather.3.cloned.1.call-start = ((), (), s32[]{:S(2)}) async-start(), calls=%async_computation | async-start | bytes 4456448 | tf_op jit(solution)/shard_map/all_gather | solution.py:22
  9.0 165.6 %all-gather.5.cloned.1.call-start = ((), (), s32[]{:S(2)}) async-start(), calls=%async_computation.1 | async-start | bytes 4456448 | tf_op jit(solution)/shard_map/all_gather | solution.py:22
  9.1 9.2 %collective-permute-start.1 = (bf16[16,64,128]{2,1,0:T(8,128)(2,1)}, bf16[16,64,128]{2,1,0:T(8,128)(2,1)S(1)}, u32[]{:S(2)}, u32[]{:S(2)}) collective-permute-start(bf16[16,64,128]{2,1,0:T(8,128)(2,1)} %convert_element_type.6), channel_id=1, source_target_pairs={{16,0},{32,16},{48,32},{64,48},{80,64},{96,80},{112,96},{128,112},... | collective-permute-start | bytes 786440 | tf_op jit(solution)/shard_map/ppermute | solution.py:14
  14.2 5.5 %collective-permute-start = (bf16[16,64,128]{2,1,0:T(8,128)(2,1)}, bf16[16,64,128]{2,1,0:T(8,128)(2,1)S(1)}, u32[]{:S(2)}, u32[]{:S(2)}) collective-permute-start(bf16[16,64,128]{2,1,0:T(8,128)(2,1)} %convert_element_type.6), channel_id=1, source_target_pairs={{0,16},{16,32},{32,48},{48,64},{64,80},{80,96},{96,112},{112,128},... | collective-permute-start | bytes 786440 | tf_op jit(solution)/shard_map/ppermute | solution.py:13
  75.5 29.1 %copy-start = (f32[1024,128]{1,0:T(8,128)S(1)}, f32[1024,128]{1,0:T(8,128)}, u32[]{:S(2)}) copy-start(f32[1024,128]{1,0:T(8,128)} %param.7) | copy-start | bytes 1572868
  118.2 342.3 %all-reduce.2.cloned.1.call-start = ((), (), s32[]{:S(2)}) async-start(), calls=%async_computation.2 | async-start | bytes 131072 | tf_op jit(solution)/shard_map/psum | solution.py:44
  118.2 8.0 %collective-permute-start.3 = (bf16[16,64,128]{2,1,0:T(8,128)(2,1)}, bf16[16,64,128]{2,1,0:T(8,128)(2,1)S(1)}, u32[]{:S(2)}, u32[]{:S(2)}) collective-permute-start(bf16[16,64,128]{2,1,0:T(8,128)(2,1)} %get-tuple-element.10), channel_id=1, source_target_pairs={{16,0},{32,16},{48,32},{64,48},{80,64},{96,80},{112,96},{128,112},... | collective-permute-start | bytes 786440 | tf_op jit(solution)/shard_map/ppermute | solution.py:14
  120.8 6.7 %collective-permute-start.2 = (bf16[16,64,128]{2,1,0:T(8,128)(2,1)}, bf16[16,64,128]{2,1,0:T(8,128)(2,1)S(1)}, u32[]{:S(2)}, u32[]{:S(2)}) collective-permute-start(bf16[16,64,128]{2,1,0:T(8,128)(2,1)} %get-tuple-element.10), channel_id=1, source_target_pairs={{0,16},{16,32},{32,48},{48,64},{64,80},{80,96},{96,112},{112,128},... | collective-permute-start | bytes 786440 | tf_op jit(solution)/shard_map/ppermute | solution.py:13
Sparse Core Ops, SparseCore 0:
  11.0 60.3 all-gather.2
  118.3 56.2 all-gather.4
  222.6 237.7 all-reduce.1
where the time goes:
time: 494 us
  waiting for transfers between devices  342 us (69%)
  local copies, waits for them, and re-layouts  60.2 us (12%)
  other arithmetic  35.5 us (7%)
  matrix products  29.3 us (6%)
  between operations  13.9 us (3%)
  starting transfers between devices  13 us (3%)
    psum x1, waiting for transfers between devices, on_device(): gram = lax.psum(local_gram, ('group', 'blk')) / rows_total  238 us
    all_gather x2, waiting for transfers between devices, couple_all(): gathered = lax.all_gather(rounded, 'blk', axis=0, tiled=True)  98.7 us
    gather x2, local copies, waits for them, and re-layouts, couple_all(): table[index.reshape(-1)]  58.3 us
    dot_general x2, matrix products, couple_all(): jnp.einsum('rsik,rskn->rin', hamiltonian, picked, preferred_element_type=...  26.3 us
    another operation x3, other arithmetic, on_device(): lower = jnp.linalg.cholesky(gram)  12.4 us
  transfers between devices with their start and end apart: 7, of which 7 were waited for; matrix products, arithmetic and copies ran while one was open for 0% of the time, Pallas kernels for 0%

commit v1 on v0

--- a/solution.py
+++ b/solution.py
@@ -19,7 +19,9 @@
     shard_blocks, nsrc, block_size, width = hamiltonian.shape
     per_source = block_columns.shape[2]
     states = rounded.shape[2]
-    gathered = lax.all_gather(rounded, "blk", axis=0, tiled=True)
+    gathered = jnp.concatenate(
+        lax.all_to_all(jnp.stack([rounded] * lax.axis_size("blk")), "blk", 0, 0), axis=0
+    )
     below, above = neighbours(rounded)
     table = jnp.concatenate([gathered, below, above], axis=0)
     offsets = (jnp.arange(nsrc, dtype=jnp.int32) * shard_blocks)[None, :, None]

time: 494 us -> 517 us (1.047)
  starting transfers between devices: 13 us -> 26 us
  waiting for transfers between devices: 342 us -> 348 us
  local copies, waits for them, and re-layouts: 60.2 us -> 65.6 us
    all_to_all x0 -> x2, waiting for transfers between devices: none -> 102 us  [couple_all(): lax.all_to_all(jnp.stack([rounded] * lax.axis_size('blk')), 'blk', 0, 0)]
    all_gather x2 -> x0, waiting for transfers between devices: 98.7 us -> none  [couple_all(): gathered = lax.all_gather(rounded, 'blk', axis=0, tiled=True)]
    all_to_all x0 -> x2, starting transfers between devices: none -> 12.2 us  [couple_all(): lax.all_to_all(jnp.stack([rounded] * lax.axis_size('blk')), 'blk', 0, 0)]
    another operation x0 -> x2, local copies, waits for them, and re-layouts: none -> 6.06 us  [couple_all(): jnp.stack([rounded] * lax.axis_size('blk'))]
where the time goes in v1:
time: 517 us; the launch traced here: 516 us
  waiting for transfers between devices  348 us (67%)
  local copies, waits for them, and re-layouts  65.6 us (13%)
  other arithmetic  34 us (7%)
  matrix products  28.6 us (6%)
  starting transfers between devices  26 us (5%)
  between operations  14.2 us (3%)
    psum x1, waiting for transfers between devices, on_device(): gram = lax.psum(local_gram, ('group', 'blk')) / rows_total  240 us
    all_to_all x2, waiting for transfers between devices, couple_all(): lax.all_to_all(jnp.stack([rounded] * lax.axis_size('blk')), 'blk', 0, 0)  102 us
    gather x2, local copies, waits for them, and re-layouts, couple_all(): table[index.reshape(-1)]  58.3 us
    dot_general x2, matrix products, couple_all(): jnp.einsum('rsik,rskn->rin', hamiltonian, picked, preferred_element_type=...  25.7 us
    another operation x3, other arithmetic, on_device(): lower = jnp.linalg.cholesky(gram)  12.4 us
    all_to_all x2, starting transfers between devices, couple_all(): lax.all_to_all(jnp.stack([rounded] * lax.axis_size('blk')), 'blk', 0, 0)  12.2 us
  transfers between devices with their start and end apart: 7, of which 7 were waited for; matrix products, arithmetic and copies ran while one was open for 0% of the time, Pallas kernels for 0%

profile of v1, /device:TPU:1, one launch (start us, length us, event | category | flops | bytes accessed | tf_op | source)
XLA Modules:
  0.0 516.1 jit_solution(8085434799348565124)
XLA Ops:
  7.2 1.1 convert_element_type.8
  8.3 3.0 stack.4
  11.3 7.6 %all-to-all-start = ((bf16[16,16,64,128]{3,2,1,0:T(8,128)(2,1)}), bf16[16,16,64,128]{3,2,1,0:T(8,128)(2,1)}, u32[]{:S(2)}, u32[]{:S(2)}) async-start(bf16[16,16,64,128]{3,2,1,0:T(8,128)(2,1)} %stack.4), calls=%async_computation | async-start | bytes 8388608 | tf_op jit(solution)/shard_map/all_to_all | solution.py:23
  19.0 2.9 collective-permute-start.1
  21.8 3.4 collective-permute-start
  25.8 2.0 collective-permute-done.1
  28.6 52.7 %all-to-all-done = bf16[16,16,64,128]{3,2,1,0:T(8,128)(2,1)} async-done(((bf16[16,16,64,128]{3,2,1,0:T(8,128)(2,1)}), bf16[16,16,64,128]{3,2,1,0:T(8,128)(2,1)}, u32[]{:S(2)}, u32[]{:S(2)}) %all-to-all-start) | async-done | bytes 4194336 | tf_op jit(solution)/shard_map/all_to_all | solution.py:23
  81.3 4.2 pad_maximum_fusion
  85.5 29.1 %gather_fusion = bf16[1152,64,128]{2,1,0:T(8,128)(2,1)} fusion(bf16[288,64,128]{2,1,0:T(8,128)(2,1)} %pad_maximum_fusion, s32[2048]{0:T(1024)S(1)} %pad_clamp_fusion), kind=kCustom, calls=%fused_computation | custom fusion | bytes 37753344 | tf_op jit(solution)/shard_map/gather | solution.py:29
  114.6 12.8 %multiply_convert_fusion = (bf16[16,64,128]{2,1,0:T(8,128)(2,1)S(1)}, f32[16,64,128]{2,1,0:T(8,128)S(1)}) fusion(f32[16,64,128]{2,1,0:T(8,128)S(1)} %bitcast.46, f32[16,64]{1,0:T(8,128)S(1)} %mul.37, bf16[16,18,64,256]{3,2,1,0:T(8,128)(2,1)} %param.4, bf16[16,18,256,128]{3,2,1,0:T(8,128)(2,1)} %bitcast.43), kind=kOutput, calls=%fused_computation.10 | convolution fusion | flops 1208483840 | bytes 29626368 | tf_op jit(solution)/shard_map/rsik,rskn->rin/dot_general | solution.py:30
  127.4 3.0 stack.5
  130.4 4.5 all-to-all-start.1
  135.0 3.8 collective-permute-start.3
  138.8 3.6 collective-permute-start.2
  142.5 2.3 collective-permute-done.3
  145.6 48.8 %all-to-all-done.1 = bf16[16,16,64,128]{3,2,1,0:T(8,128)(2,1)} async-done(((bf16[16,16,64,128]{3,2,1,0:T(8,128)(2,1)}), bf16[16,16,64,128]{3,2,1,0:T(8,128)(2,1)}, u32[]{:S(2)}, u32[]{:S(2)}) %all-to-all-start.1) | async-done | bytes 4194336 | tf_op jit(solution)/shard_map/all_to_all | solution.py:23
  194.4 4.2 pad_maximum_fusion.1
  198.6 29.2 %gather_fusion.1 = bf16[1152,64,128]{2,1,0:T(8,128)(2,1)} fusion(bf16[288,64,128]{2,1,0:T(8,128)(2,1)} %pad_maximum_fusion.1, s32[2048]{0:T(1024)S(1)} %pad_clamp_fusion), kind=kCustom, calls=%fused_computation.1 | custom fusion | bytes 37753344 | tf_op jit(solution)/shard_map/gather | solution.py:29
  227.8 12.8 %fusion.2 = f32[16,64,128]{2,1,0:T(8,128)S(1)} fusion(f32[16,64,128]{2,1,0:T(8,128)S(1)} %bitcast.47, bf16[16,18,64,256]{3,2,1,0:T(8,128)(2,1)} %param.4, bf16[16,18,256,128]{3,2,1,0:T(8,128)(2,1)} %bitcast.42, f32[16,64,128]{2,1,0:T(8,128)S(1)} %get-tuple-element.9, f32[16,64]{1,0:T(8,128)S(1)} %broadcast_multiply_fusion.1), kind=kOutput, calls=%fused_computation.8 | convolution fusion | flops 1208352768 | bytes 29888512 | tf_op jit(solution)/shard_map/rsik,rskn->rin/dot_general | solution.py:30
  240.6 1.6 convolution_bitcast_fusion.2
  242.3 240.2 %all-reduce.2.cloned.1.call-done = f32[128,128]{0,1:T(8,128)} async-done(((f32[128,128]{0,1:T(8,128)}), f32[128,128]{0,1:T(8,128)}) %all-reduce.2.cloned.1.call-update) | async-done | bytes 65552 | tf_op jit(solution)/shard_map/psum | solution.py:46
  484.3 11.7 %cholesky.16 = f32[128,128]{1,0:T(8,128)S(1)} custom-call(f32[128,128]{1,0:T(8,128)S(1)} %fusion.5), custom_call_target="Cholesky" | custom-call | tf_op jit(solution)/shard_map/jit(cholesky)/cholesky | solution.py:47
  498.1 9.8 %custom-call.6 = f32[1,128,128]{1,2,0:T(8,128)S(1)} custom-call(f32[1,128,128]{2,1,0:T(8,128)S(1)} %get-tuple-element.7), custom_call_target="InvertDiagBlocksLowerTriangular" | custom-call | tf_op jit(solution)/shard_map/triangular_solve | solution.py:48
  507.9 1.4 fusion.3
  (25 shorter events, 6.0 us)
Async XLA Ops:
  7.2 18.1 %copy-start.1 = (s32[16,18,4]{1,2,0:T(4,128)S(1)}, s32[16,18,4]{1,2,0:T(4,128)}, u32[]{:S(2)}) copy-start(s32[16,18,4]{1,2,0:T(4,128)} %param.5) | copy-start | bytes 13828
  7.2 18.1 %copy-start.2 = (f32[1024]{0:T(1024)S(1)}, f32[1024]{0:T(1024)}, u32[]{:S(2)}) copy-start(f32[1024]{0:T(1024)} %param.6) | copy-start | bytes 12292
  11.3 70.0 %all-to-all-start = ((bf16[16,16,64,128]{3,2,1,0:T(8,128)(2,1)}), bf16[16,16,64,128]{3,2,1,0:T(8,128)(2,1)}, u32[]{:S(2)}, u32[]{:S(2)}) async-start(bf16[16,16,64,128]{3,2,1,0:T(8,128)(2,1)} %stack.4), calls=%async_computation | async-start | bytes 8388608 | tf_op jit(solution)/shard_map/all_to_all | solution.py:23
  19.0 8.8 %collective-permute-start.1 = (bf16[16,64,128]{2,1,0:T(8,128)(2,1)S(1)}, bf16[16,64,128]{2,1,0:T(8,128)(2,1)S(1)}, u32[]{:S(2)}, u32[]{:S(2)}) collective-permute-start(bf16[16,64,128]{2,1,0:T(8,128)(2,1)S(1)} %convert_element_type.8), channel_id=1, source_target_pairs={{16,0},{32,16},{48,32},{64,48},{80,64},{96,80},{112,96},{128,112},... | collective-permute-start | bytes 786440 | tf_op jit(solution)/shard_map/ppermute | solution.py:14
  21.8 6.7 %collective-permute-start = (bf16[16,64,128]{2,1,0:T(8,128)(2,1)S(1)}, bf16[16,64,128]{2,1,0:T(8,128)(2,1)S(1)}, u32[]{:S(2)}, u32[]{:S(2)}) collective-permute-start(bf16[16,64,128]{2,1,0:T(8,128)(2,1)S(1)} %convert_element_type.8), channel_id=1, source_target_pairs={{0,16},{16,32},{32,48},{48,64},{64,80},{80,96},{96,112},{112,128},... | collective-permute-start | bytes 786440 | tf_op jit(solution)/shard_map/ppermute | solution.py:13
  85.5 29.1 %copy-start = (f32[1024,128]{1,0:T(8,128)S(1)}, f32[1024,128]{1,0:T(8,128)}, u32[]{:S(2)}) copy-start(f32[1024,128]{1,0:T(8,128)} %param.7) | copy-start | bytes 1572868
  130.4 64.0 %all-to-all-start.1 = ((bf16[16,16,64,128]{3,2,1,0:T(8,128)(2,1)}), bf16[16,16,64,128]{3,2,1,0:T(8,128)(2,1)}, u32[]{:S(2)}, u32[]{:S(2)}) async-start(bf16[16,16,64,128]{3,2,1,0:T(8,128)(2,1)} %stack.5), calls=%async_computation.1 | async-start | bytes 8388608 | tf_op jit(solution)/shard_map/all_to_all | solution.py:23
  135.0 347.6 %all-reduce.2.cloned.1.call-start = ((), (), s32[]{:S(2)}) async-start(), calls=%async_computation.2 | async-start | bytes 131072 | tf_op jit(solution)/shard_map/psum | solution.py:46
  135.0 9.8 %collective-permute-start.3 = (bf16[16,64,128]{2,1,0:T(8,128)(2,1)S(1)}, bf16[16,64,128]{2,1,0:T(8,128)(2,1)S(1)}, u32[]{:S(2)}, u32[]{:S(2)}) collective-permute-start(bf16[16,64,128]{2,1,0:T(8,128)(2,1)S(1)} %get-tuple-element.8), channel_id=1, source_target_pairs={{16,0},{32,16},{48,32},{64,48},{80,64},{96,80},{112,96},{128,112},... | collective-permute-start | bytes 786440 | tf_op jit(solution)/shard_map/ppermute | solution.py:14
  138.8 6.8 %collective-permute-start.2 = (bf16[16,64,128]{2,1,0:T(8,128)(2,1)S(1)}, bf16[16,64,128]{2,1,0:T(8,128)(2,1)S(1)}, u32[]{:S(2)}, u32[]{:S(2)}) collective-permute-start(bf16[16,64,128]{2,1,0:T(8,128)(2,1)S(1)} %get-tuple-element.8), channel_id=1, source_target_pairs={{0,16},{16,32},{32,48},{48,64},{64,80},{80,96},{96,112},{112,128},... | collective-permute-start | bytes 786440 | tf_op jit(solution)/shard_map/ppermute | solution.py:13
Sparse Core Ops, SparseCore 0:
  242.4 240.0 all-reduce.1
